TPU v7x, 128 devices: a whole 4x4x4 slice. The times are simulated.
128 devices in a mesh: row: 16 (over x, z), col: 8 (over y, core).
Axes of the slice: x: 4, y: 4, z: 4, core: 2. Of those that a mesh axis runs over, the one named last changes fastest.
Arguments:
- qkv: bfloat16 [3, 1408, 32768], P(None, 'col', 'row'), may hold values from -12.1 to 12.1
- residual_in: bfloat16 [1408, 32768], P('col', 'row'), may hold values from -3 to 3
- out_weight: bfloat16 [1408, 1408], replicated, may hold values from -0.625 to 0.625
- merge_weight: bfloat16 [1408, 5632], P('col'), may hold values from -0.078125 to 0.078125
- merge_gain: float32 [1408], replicated, may hold values from 0.1 to 1.9
- image_groups: int32 [64], replicated, may hold values from 1 to 256, 8192 in all
- dest_row: int32 [8192], P('row'), may hold values from 0 to 8191, as said below
Outputs:
- layer_out: bfloat16 [1408, 32768], P('col', 'row')
- image_rows: bfloat16 [1408, 8192], P('col', 'row')
Inputs may be any that keep to these rules, and one draw needn't show every extreme that they name: dest_row is a permutation of 0 to 8191. Of the 512 entries held by each index of row, exactly 32 fall in each aligned block of 512 output rows.
All inputs are finite; a program needn't handle non-finite values.
Results may differ from a plain program's by a relative error of at most 0.0064.
Values may be sent and summed in bfloat16 or wider, within the bound.
A program may use at most 128 MiB of HBM per device.

v0:
```python
import math
import jax
import jax.numpy as jnp
from jax import lax
from jax.sharding import PartitionSpec as P

HEAD_DIM = 88


def with_halo(cells, sides, width):
    for axis, dim in sides:
        count = lax.axis_size(axis)
        ends = count - 1
        head = lax.slice_in_dim(cells, 0, width, axis=dim)
        tail = lax.slice_in_dim(cells, cells.shape[dim] - width, cells.shape[dim], axis=dim)
        cells = jnp.concatenate(
            [
                lax.ppermute(tail, axis, [(i, (i + 1) % count) for i in range(ends)]),
                cells,
                lax.ppermute(head, axis, [((i + 1) % count, i) for i in range(ends)]),
            ],
            axis=dim,
        )
    return cells


def image_labels(positions, image_ends, all_tokens):
    inside = (positions >= 0) & (positions < all_tokens)
    counted = jnp.sum((positions[:, None] >= image_ends[None, :]).astype(jnp.int32), axis=1)
    return jnp.where(inside, counted, -1)


def body(qkv, residual_in, out_weight, merge_weight, merge_gain, image_groups, dest_row):
    width_here = qkv.shape[1]
    tok_rows = qkv.shape[2]
    heads_here = width_here // HEAD_DIM
    full_width = out_weight.shape[0]
    reach_rows = tok_rows // 2
    block_rows = min(1024, tok_rows)
    block_count = tok_rows // block_rows
    window = block_rows + 2 * reach_rows
    row_count = lax.axis_size("row")
    row_id = lax.axis_index("row")
    col_id = lax.axis_index("col")
    all_tokens = tok_rows * row_count
    score_scale = 1.0 / math.sqrt(HEAD_DIM)
    image_ends = jnp.cumsum(image_groups) * 4
    extended = with_halo(qkv[1:], (("row", 2),), reach_rows)
    positions = (
        row_id * tok_rows - reach_rows + jnp.arange(tok_rows + 2 * reach_rows, dtype=jnp.int32)
    )
    labels = image_labels(positions, image_ends, all_tokens)

    def attend(block_id):
        first_row = block_id * block_rows
        queries = lax.dynamic_slice_in_dim(qkv[0], first_row, block_rows, 1).reshape(
            heads_here, HEAD_DIM, block_rows
        )
        key_block = lax.dynamic_slice_in_dim(extended[0], first_row, window, 1).reshape(
            heads_here, HEAD_DIM, window
        )
        value_block = lax.dynamic_slice_in_dim(extended[1], first_row, window, 1).reshape(
            heads_here, HEAD_DIM, window
        )
        query_labels = lax.dynamic_slice_in_dim(labels, first_row + reach_rows, block_rows, 0)
        key_labels = lax.dynamic_slice_in_dim(labels, first_row, window, 0)
        scores = (
            jnp.einsum("hdq,hdk->hqk", queries, key_block, preferred_element_type=jnp.float32)
            * score_scale
        )
        same_image = (query_labels[:, None] == key_labels[None, :])[None]
        scores = jnp.where(same_image, scores, -1e30)
        row_max = jnp.max(scores, axis=2, keepdims=True)
        exponent = jnp.exp(scores - row_max)
        totals = jnp.sum(exponent, axis=2)
        weights = exponent.astype(jnp.bfloat16)
        weighted = jnp.einsum(
            "hqk,hdk->hdq", weights, value_block, preferred_element_type=jnp.float32
        )
        weighted = weighted / totals[:, None, :]
        return weighted.astype(jnp.bfloat16).reshape(width_here, block_rows)

    attended = lax.map(attend, jnp.arange(block_count, dtype=jnp.int32))
    attended = jnp.transpose(attended, (1, 0, 2)).reshape(width_here, tok_rows)
    head_weight = lax.dynamic_slice_in_dim(out_weight, col_id * width_here, width_here, 0)
    partial_value = lax.dot_general(
        head_weight, attended, (((0,), (0,)), ((), ())), preferred_element_type=jnp.float32
    )
    projected = lax.psum_scatter(partial_value, "col", scatter_dimension=0, tiled=True)
    layer_out = (residual_in.astype(jnp.float32) + projected).astype(jnp.bfloat16)
    full_rows = lax.all_gather(layer_out, "col", axis=0, tiled=True)
    values32 = full_rows.astype(jnp.float32)
    centre = jnp.mean(values32, axis=0, keepdims=True)
    spread = jnp.mean(jnp.square(values32 - centre), axis=0, keepdims=True)
    normed = ((values32 - centre) * lax.rsqrt(spread + 1e-06) * merge_gain[:, None]).astype(
        jnp.bfloat16
    )
    group_rows = tok_rows // 4
    grouped = normed.reshape(full_width, group_rows, 4)
    weight_parts = merge_weight.reshape(width_here, 4, full_width)
    merged = jnp.einsum(
        "ojf,fgj->og", weight_parts, grouped, preferred_element_type=jnp.float32
    ).astype(jnp.bfloat16)
    empty_rows = jnp.zeros((width_here, group_rows), jnp.bfloat16)
    every_row, every_dest = (
        lax.all_gather(merged, "row", axis=1, tiled=True),
        lax.all_gather(dest_row, "row", axis=0, tiled=True),
    )
    slot_index = every_dest - row_id * group_rows
    slot_index = jnp.where((slot_index >= 0) & (slot_index < group_rows), slot_index, group_rows)
    image_rows = empty_rows.at[:, slot_index].set(every_row, mode="drop")
    return (layer_out, image_rows)


def solution(mesh):
    return jax.shard_map(
        body,
        mesh=mesh,
        in_specs=(P(None, "col", "row"), P("col", "row"), P(), P("col", None), P(), P(), P("row")),
        out_specs=(P("col", "row"), P("col", "row")),
        check_vma=False,
    )
```

profile of v0, /device:TPU:0, one launch (start us, length us, event | category | flops | bytes accessed | tf_op | source)
XLA Modules:
  0.0 381.6 jit_solution(7010875313808431647)
XLA Ops:
  7.2 2.4 fusion.44
  9.7 3.9 %collective-permute-start = (bf16[2,176,1024]{2,1,0:T(8,128)(2,1)}, bf16[2,176,1024]{2,1,0:T(8,128)(2,1)S(1)}, u32[]{:S(2)}, u32[]{:S(2)}) collective-permute-start(bf16[2,176,1024]{2,1,0:T(8,128)(2,1)} %get-tuple-element.106), channel_id=1, source_target_pairs={{0,8},{8,16},{16,24},{24,32},{32,40},{40,48},{48,56},{56,64},{64,7... | collective-permute-start | bytes 2162696 | tf_op jit(solution)/shard_map/ppermute | solution.py:18
  13.6 1.3 collective-permute-start.1
  15.0 0.1 copy.28
  15.1 0.1 reduce-window.8
  15.2 0.1 multiply_reduce_fusion
  15.3 0.2 convert_reduce_fusion.1
  15.5 13.8 %collective-permute-done = bf16[2,176,1024]{2,1,0:T(8,128)(2,1)S(1)} collective-permute-done((bf16[2,176,1024]{2,1,0:T(8,128)(2,1)}, bf16[2,176,1024]{2,1,0:T(8,128)(2,1)S(1)}, u32[]{:S(2)}, u32[]{:S(2)}) %collective-permute-start) | collective-permute-done | bytes 720928 | tf_op jit(solution)/shard_map/ppermute | solution.py:18
  29.3 4.1 %collective-permute-done.1 = bf16[2,176,1024]{2,1,0:T(8,128)(2,1)} collective-permute-done((bf16[2,176,1024]{2,1,0:T(8,128)(2,1)S(1)}, bf16[2,176,1024]{2,1,0:T(8,128)(2,1)}, u32[]{:S(2)}, u32[]{:S(2)}) %collective-permute-start.1) | collective-permute-done | bytes 720928 | tf_op jit(solution)/shard_map/ppermute | solution.py:20
  33.4 3.1 pad_maximum_fusion
  36.4 91.2 %while.12 = (s32[]{:T(128)}, bf16[2,176,1024]{2,1,0:T(8,128)(2,1)}, bf16[2,176,4096]{2,1,0:T(8,128)(2,1)}, s32[2]{0:T(128)S(1)}, s32[4096]{0:T(1024)S(1)}, /*ind...) while((s32[]{:T(128)}, bf16[2,176,1024]{2,1,0:T(8,128)(2,1)}, ...), condition=%wide.region_5.6_spmd, body=%wide.region_2.5_spmd.sunk | while | flops 2287300608 | bytes 108356392 | solution.py:83
  36.4 0.7 dynamic_slice.44
  37.8 2.0 broadcast_compare_fusion.2
  39.8 2.1 fusion.61
  41.9 1.6 constant_dynamic-slice_fusion.5
  43.6 1.2 slice.41
  44.8 12.6 %fusion.62 = (f32[2,1024]{1,0:T(2,128)S(1)}, f32[2,1024,3072]{2,1,0:T(8,128)}) fusion(pred[1024,3072]{1,0:T(8,128)(4,1)S(1)} %broadcast_compare_fusion.2, bf16[2,88,1024]{2,1,0:T(8,128)(2,1)S(1)} %bitcast.59, bf16[2,88,3072]{2,1,0:T(8,128)(2,1)} %bitcast.57), kind=kOutput, calls=%fused_computation.3.clone.1 | convolution fusion | flops 1126168576 | bytes 29761536 | tf_op jit(solution)/shard_map/while/body/eval_jaxpr/hdq,hdk->hqk/dot_general | solution.py:68
  57.4 12.0 %fusion.63 = f32[2,1024]{1,0:T(2,128)S(1)} fusion(f32[2,1024,3072]{2,1,0:T(8,128)} %get-tuple-element.155, f32[2,1024]{1,0:T(2,128)S(1)} %get-tuple-element.156, pred[1024,3072]{1,0:T(8,128)(4,1)S(1)} %broadcast_compare_fusion.2), kind=kLoop, calls=%fused_computation.4.clone.1 | loop fusion | flops 25163776 | bytes 28327936 | tf_op jit(solution)/shard_map/while/body/eval_jaxpr/reduce_sum | solution.py:75
  69.4 11.8 %fusion.64 = bf16[2,88,1024]{2,1,0:T(8,128)(2,1)S(1)} fusion(bf16[2,88,3072]{2,1,0:T(8,128)(2,1)S(1)} %bitcast.56, f32[2,1024,3072]{2,1,0:T(8,128)} %get-tuple-element.155, f32[2,1024]{1,0:T(2,128)S(1)} %get-tuple-element.156, pred[1024,3072]{1,0:T(8,128)(4,1)S(1)} %broadcast_compare_fusion.2, f32[2,1024]{1,0:T(2,128)S(1)} %fusion.63), kind=kOutput, calls=%fused_computation.10.clone.1 | convolution fusion | flops 1132822528 | bytes 29769728 | tf_op jit(solution)/shard_map/while/body/eval_jaxpr/hqk,hdk->hdq/dot_general | solution.py:77
  81.3 0.8 bitcast_dynamic-update-slice_fusion.2
  82.0 0.7 dynamic_slice.44
  83.4 2.0 broadcast_compare_fusion.2
  85.4 2.1 fusion.61
  87.5 1.6 constant_dynamic-slice_fusion.5
  89.2 1.2 slice.41
  90.4 12.6 %fusion.62 = (f32[2,1024]{1,0:T(2,128)S(1)}, f32[2,1024,3072]{2,1,0:T(8,128)}) fusion(pred[1024,3072]{1,0:T(8,128)(4,1)S(1)} %broadcast_compare_fusion.2, bf16[2,88,1024]{2,1,0:T(8,128)(2,1)S(1)} %bitcast.59, bf16[2,88,3072]{2,1,0:T(8,128)(2,1)} %bitcast.57), kind=kOutput, calls=%fused_computation.3.clone.1 | convolution fusion | flops 1126168576 | bytes 29761536 | tf_op jit(solution)/shard_map/while/body/eval_jaxpr/hdq,hdk->hqk/dot_general | solution.py:68
  103.0 12.0 %fusion.63 = f32[2,1024]{1,0:T(2,128)S(1)} fusion(f32[2,1024,3072]{2,1,0:T(8,128)} %get-tuple-element.155, f32[2,1024]{1,0:T(2,128)S(1)} %get-tuple-element.156, pred[1024,3072]{1,0:T(8,128)(4,1)S(1)} %broadcast_compare_fusion.2), kind=kLoop, calls=%fused_computation.4.clone.1 | loop fusion | flops 25163776 | bytes 28327936 | tf_op jit(solution)/shard_map/while/body/eval_jaxpr/reduce_sum | solution.py:75
  115.0 11.8 %fusion.64 = bf16[2,88,1024]{2,1,0:T(8,128)(2,1)S(1)} fusion(bf16[2,88,3072]{2,1,0:T(8,128)(2,1)S(1)} %bitcast.56, f32[2,1024,3072]{2,1,0:T(8,128)} %get-tuple-element.155, f32[2,1024]{1,0:T(2,128)S(1)} %get-tuple-element.156, pred[1024,3072]{1,0:T(8,128)(4,1)S(1)} %broadcast_compare_fusion.2, f32[2,1024]{1,0:T(2,128)S(1)} %fusion.63), kind=kOutput, calls=%fused_computation.10.clone.1 | convolution fusion | flops 1132822528 | bytes 29769728 | tf_op jit(solution)/shard_map/while/body/eval_jaxpr/hqk,hdk->hdq/dot_general | solution.py:77
  126.9 0.8 bitcast_dynamic-update-slice_fusion.2
  127.7 1.2 copy.36
  128.8 7.1 %fusion.38 = f32[1408,2048]{1,0:T(8,128)} fusion(bf16[176,2048]{1,0:T(8,128)(2,1)S(1)} %bitcast.61, bf16[1408,1408]{1,0:T(8,128)(2,1)} %param.11, s32[]{:T(128)S(6)} %select_n.41), kind=kOutput, calls=%fused_computation.34 | convolution fusion | flops 1015021568 | bytes 12750852 | tf_op jit(solution)/shard_map/dot_general | solution.py:86
  135.9 0.2 all-gather.4.cloned.1.call-start
  136.2 70.0 %reduce-scatter.2.cloned.1.call-done = f32[176,2048]{1,0:T(8,128)} async-done(((f32[1408,2048]{1,0:T(8,128)}), f32[176,2048]{1,0:T(8,128)}) %reduce-scatter.2.cloned.1.call-update) | async-done | bytes 1441808 | tf_op jit(solution)/shard_map/reduce_scatter | solution.py:89
  206.2 2.4 add_convert_fusion
  208.6 0.0 all-gather.6.cloned.1.call-start
  208.7 38.4 %all-gather.4.cloned.1.call-done = bf16[1408,2048]{1,0:T(8,128)(2,1)} async-done(((bf16[176,2048]{1,0:T(8,128)(2,1)}), bf16[1408,2048]{1,0:T(8,128)(2,1)}) %all-gather.4.cloned.1.call-update) | async-done | bytes 5767184 | tf_op jit(solution)/shard_map/all_gather | solution.py:91
  247.1 3.7 convert_reduce_fusion
  250.8 0.6 copy-done
  251.4 1.5 fusion.16
  253.0 4.3 %fusion.18 = bf16[1408,2048]{1,0:T(8,128)(2,1)} fusion(bf16[1408,2048]{1,0:T(8,128)(2,1)S(1)} %copy-done, f32[1408]{0:T(1024)S(1)} %copy-done.3, f32[2048]{0:T(1024)S(1)} %add_rsqrt_fusion, f32[2048]{0:T(1024)S(1)} %broadcast_multiply_fusion), kind=kLoop, calls=%fused_computation.23 | loop fusion | flops 14417920 | bytes 11556352 | tf_op jit(solution)/shard_map/convert_element_type | solution.py:95
  257.2 8.4 %copy.30 = bf16[1408,2048]{0,1:T(8,128)(2,1)} copy(bf16[1408,2048]{1,0:T(8,128)(2,1)} %fusion.18) | data formatting | bytes 11534336 | tf_op jit(solution)/shard_map/convert_element_type | solution.py:95
  265.6 10.6 %reshape.116 = bf16[1408,512,4]{0,2,1:T(4,128)(2,1)} reshape(bf16[1408,2048]{0,1:T(8,128)(2,1)} %copy.30) | data formatting | bytes 11534336 | tf_op jit(solution)/shard_map/reshape | solution.py:99
  276.2 5.4 %fusion.33 = bf16[176,512]{1,0:T(8,128)(2,1)} fusion(bf16[1408,512,4]{0,2,1:T(4,128)(2,1)} %reshape.116, bf16[22,4,8,1408]{3,2,1,0:T(8,128)(2,1)S(1)} %bitcast.67), kind=kOutput, calls=%fused_computation.32 | convolution fusion | flops 1015111680 | bytes 7929856 | tf_op jit(solution)/shard_map/ojf,fgj->og/dot_general | solution.py:101
  281.7 23.5 %all-gather = s32[16,1,512]{2,1,0:T(1,128)S(1)} all-gather(s32[1,1,512]{2,1,0:T(1,128)S(1)} %bitcast.65), channel_id=1, replica_groups=mesh['row'=16,'col'=8] {'row'}, dimensions={0}, use_global_device_ids=true | all-gather | bytes 34816 | tf_op jit(solution)/shard_map/all_gather | solution.py:107
  305.2 28.1 %all-gather.6.cloned.1.call-done = bf16[176,8192]{1,0:T(8,128)(2,1)} async-done(((bf16[176,512]{1,0:T(8,128)(2,1)}), bf16[176,8192]{1,0:T(8,128)(2,1)}) %all-gather.6.cloned.1.call-update) | async-done | bytes 2883600 | tf_op jit(solution)/shard_map/all_gather | solution.py:106
  333.3 5.8 %copy.33 = bf16[8192,176]{1,0:T(8,128)(2,1)} copy(bf16[8192,176]{0,1:T(8,128)(2,1)} %bitcast.60) | data formatting | bytes 5767168 | tf_op jit(solution)/shard_map/all_gather | solution.py:106
  339.1 35.2 %scatter_custom_fusion = bf16[176,512]{0,1:T(8,128)(2,1)S(1)} fusion(s32[8192]{0:T(1024)S(1)} %compare_select_fusion, bf16[8192,176]{1,0:T(8,128)(2,1)} %copy.33, bf16[]{:T(256)} %constant.97.clone.1), kind=kCustom, calls=%fused_computation.36 | custom fusion | bytes 180736 | tf_op jit(solution)/shard_map/scatter | solution.py:111
  374.3 0.8 copy.34
  (35 shorter events, 0.3 us)
Async XLA Ops:
  7.2 26.2 %slice-start = ((bf16[3,176,2048]{2,1,0:T(8,128)(2,1)}), bf16[2,176,2048]{2,1,0:T(8,128)(2,1)S(1)}, s32[]{:S(2)}) async-start(bf16[3,176,2048]{2,1,0:T(8,128)(2,1)} %param.9), calls=%async_computation.4 | async-start | bytes 2883584 | tf_op jit(solution)/shard_map/slice | solution.py:48
  7.2 7.8 %copy-start.5 = (s32[64]{0:T(128)S(1)}, s32[64]{0:T(128)}, u32[]{:S(2)}) copy-start(s32[64]{0:T(128)} %param.14) | copy-start | bytes 772
  7.2 199.0 %reduce-scatter.2.cloned.1.call-start = ((), (), s32[]{:S(2)}) async-start(), calls=%async_computation.1 | async-start | bytes 12976128 | tf_op jit(solution)/shard_map/reduce_scatter | solution.py:89
  9.7 19.6 %collective-permute-start = (bf16[2,176,1024]{2,1,0:T(8,128)(2,1)}, bf16[2,176,1024]{2,1,0:T(8,128)(2,1)S(1)}, u32[]{:S(2)}, u32[]{:S(2)}) collective-permute-start(bf16[2,176,1024]{2,1,0:T(8,128)(2,1)} %get-tuple-element.106), channel_id=1, source_target_pairs={{0,8},{8,16},{16,24},{24,32},{32,40},{40,48},{48,56},{56,64},{64,7... | collective-permute-start | bytes 2162696 | tf_op jit(solution)/shard_map/ppermute | solution.py:18
  13.6 19.7 %collective-permute-start.1 = (bf16[2,176,1024]{2,1,0:T(8,128)(2,1)S(1)}, bf16[2,176,1024]{2,1,0:T(8,128)(2,1)}, u32[]{:S(2)}, u32[]{:S(2)}) collective-permute-start(bf16[2,176,1024]{2,1,0:T(8,128)(2,1)S(1)} %get-tuple-element.107), channel_id=1, source_target_pairs={{8,0},{16,8},{24,16},{32,24},{40,32},{48,40},{56,48},{64,56},{72,6... | collective-permute-start | bytes 2162696 | tf_op jit(solution)/shard_map/ppermute | solution.py:20
  57.4 12.0 %copy-start.1 = (bf16[1,176,3072]{2,1,0:T(8,128)(2,1)S(1)}, bf16[1,176,3072]{2,1,0:T(8,128)(2,1)}, u32[]{:S(2)}) copy-start(bf16[1,176,3072]{2,1,0:T(8,128)(2,1)} %get-tuple-element.153) | copy-start | bytes 3244036 | tf_op jit(solution)/shard_map/while
  103.0 12.0 %copy-start.1 = (bf16[1,176,3072]{2,1,0:T(8,128)(2,1)S(1)}, bf16[1,176,3072]{2,1,0:T(8,128)(2,1)}, u32[]{:S(2)}) copy-start(bf16[1,176,3072]{2,1,0:T(8,128)(2,1)} %get-tuple-element.153) | copy-start | bytes 3244036 | tf_op jit(solution)/shard_map/while
  135.9 70.3 %copy-start.2 = (bf16[176,2048]{1,0:T(8,128)(2,1)S(1)}, bf16[176,2048]{1,0:T(8,128)(2,1)}, u32[]{:S(2)}) copy-start(bf16[176,2048]{1,0:T(8,128)(2,1)} %param.10) | copy-start | bytes 2162692
  135.9 111.1 %all-gather.4.cloned.1.call-start = ((), (), s32[]{:S(2)}) async-start(), calls=%async_computation.2 | async-start | bytes 6488064 | tf_op jit(solution)/shard_map/all_gather | solution.py:91
  208.6 44.3 %copy-start.3 = (f32[1408]{0:T(1024)S(1)}, f32[1408]{0:T(1024)}, u32[]{:S(2)}) copy-start(f32[1408]{0:T(1024)} %param.13) | copy-start | bytes 16900
  208.6 124.7 %all-gather.6.cloned.1.call-start = ((), (), s32[]{:S(2)}) async-start(), calls=%async_computation.3 | async-start | bytes 3063808 | tf_op jit(solution)/shard_map/all_gather | solution.py:106
  247.1 4.3 %copy-start = (bf16[1408,2048]{1,0:T(8,128)(2,1)S(1)}, bf16[1408,2048]{1,0:T(8,128)(2,1)}, u32[]{:S(2)}) copy-start(bf16[1408,2048]{1,0:T(8,128)(2,1)} %all-gather.4.cloned.1.call-done) | copy-start | bytes 17301508
  265.6 10.7 %copy-start.6 = (bf16[176,5632]{1,0:T(8,128)(2,1)S(1)}, bf16[176,5632]{1,0:T(8,128)(2,1)}, u32[]{:S(2)}) copy-start(bf16[176,5632]{1,0:T(8,128)(2,1)} %param.12) | copy-start | bytes 5947396
  276.2 5.4 %copy-start.4 = (s32[512]{0:T(512)S(1)}, s32[512]{0:T(512)}, u32[]{:S(2)}) copy-start(s32[512]{0:T(512)} %param.15) | copy-start | bytes 6148
Sparse Core Ops, SparseCore 0:
  136.1 70.0 reduce-scatter.1
  208.7 38.2 all-gather.3
  281.8 51.4 all-gather.5
where the time goes:
time: 383 us; the launch traced here: 382 us
  waiting for transfers between devices  154 us (40%)
  local copies, waits for them, and re-layouts  77.9 us (20%)
  matrix products  61.4 us (16%)
  other arithmetic  43.4 us (11%)
  blocking collectives  23.5 us (6%)
  between operations  13.9 us (4%)
  starting transfers between devices  5.53 us (1%)
    reduce_scatter x1, waiting for transfers between devices, body(): lax.psum_scatter(partial_value, 'col', scatter_dimension=0, tiled=True)  70 us
    all_gather x1, waiting for transfers between devices, body(): full_rows = lax.all_gather(layer_out, 'col', axis=0, tiled=True)  38.4 us
    scatter x1, local copies, waits for them, and re-layouts, body(): image_rows = empty_rows.at[:, slot_index].set(every_row, mode='drop')  35.2 us
    all_gather x1, waiting for transfers between devices, body(): lax.all_gather(merged, 'row', axis=1, tiled=True)  28.1 us
    dot_general x2, matrix products, attend(): jnp.einsum('hdq,hdk->hqk', queries, key_block, preferred_element_type=jnp...  25.3 us
    reduce_sum x2, other arithmetic, attend(): totals = jnp.sum(exponent, axis=2)  24 us
    dot_general x2, matrix products, attend(): jnp.einsum('hqk,hdk->hdq', weights, value_block, preferred_element_type=j...  23.7 us
    all_gather x1, blocking collectives, body(): lax.all_gather(dest_row, 'row', axis=0, tiled=True)  23.5 us
  transfers between devices with their start and end apart: 5, of which 5 were waited for; matrix products, arithmetic and copies ran while one was open for 0% of the time, Pallas kernels for 0%

commit v1 on v0

--- a/solution.py
+++ b/solution.py
@@ -5,6 +5,16 @@
 from jax.sharding import PartitionSpec as P
 
 HEAD_DIM = 88
+
+
+def _end_weights(xx):
+    u1 = jnp.concatenate(
+        lax.all_to_all(
+            jnp.stack(lax.axis_size("row") * [xx], 0), axis_name="row", concat_axis=0, split_axis=0
+        ),
+        1,
+    )
+    return u1
 
 
 def with_halo(cells, sides, width):
@@ -103,7 +113,7 @@
     ).astype(jnp.bfloat16)
     empty_rows = jnp.zeros((width_here, group_rows), jnp.bfloat16)
     every_row, every_dest = (
-        lax.all_gather(merged, "row", axis=1, tiled=True),
+        _end_weights(merged),
         lax.all_gather(dest_row, "row", axis=0, tiled=True),
     )
     slot_index = every_dest - row_id * group_rows

time: 383 us -> 399 us (1.042)
  blocking collectives: 23.5 us -> 56.2 us
  waiting for transfers between devices: 154 us -> 126 us
  starting transfers between devices: 5.53 us -> 12.4 us
    all_gather x1, blocking collectives: 23.5 us -> 56.2 us  [body(): lax.all_gather(dest_row, 'row', axis=0, tiled=True)]
    all_gather x1 -> x0, waiting for transfers between devices: 28.1 us -> none  [body(): lax.all_gather(merged, 'row', axis=1, tiled=True)]
    all_to_all x0 -> x1, starting transfers between devices: none -> 6.94 us  [_end_weights(): lax.all_to_all(jnp.stack(lax.axis_size('row') * [xx], 0), axis_name='row'...]
    reshape x0 -> x2, local copies, waits for them, and re-layouts: none -> 6.02 us  [_end_weights(): jnp.concatenate(lax.all_to_all(jnp.stack(lax.axis_size('row') * [xx], 0),...]
    all_gather x1 -> x0, local copies, waits for them, and re-layouts: 5.8 us -> none  [body(): lax.all_gather(merged, 'row', axis=1, tiled=True)]
  transfers between devices with their start and end apart: 5 -> 5, of which waited for: 5 -> 4; matrix products, arithmetic and copies ran while one was open for 0% -> 0% of each run, Pallas kernels for 0% -> 0%
where the time goes in v1:
time: 399 us; the launch traced here: 396 us
  waiting for transfers between devices  126 us (32%)
  local copies, waits for them, and re-layouts  81.5 us (20%)
  matrix products  60.8 us (15%)
  blocking collectives  56.2 us (14%)
  other arithmetic  43.4 us (11%)
  between operations  14.2 us (4%)
  starting transfers between devices  12.4 us (3%)
    reduce_scatter x1, waiting for transfers between devices, body(): lax.psum_scatter(partial_value, 'col', scatter_dimension=0, tiled=True)  70 us
    all_gather x1, blocking collectives, body(): lax.all_gather(dest_row, 'row', axis=0, tiled=True)  56.2 us
    all_gather x1, waiting for transfers between devices, body(): full_rows = lax.all_gather(layer_out, 'col', axis=0, tiled=True)  38.4 us
    scatter x1, local copies, waits for them, and re-layouts, body(): image_rows = empty_rows.at[:, slot_index].set(every_row, mode='drop')  35.2 us
    dot_general x2, matrix products, attend(): jnp.einsum('hdq,hdk->hqk', queries, key_block, preferred_element_type=jnp...  25.3 us
    reduce_sum x2, other arithmetic, attend(): totals = jnp.sum(exponent, axis=2)  24 us
    dot_general x2, matrix products, attend(): jnp.einsum('hqk,hdk->hdq', weights, value_block, preferred_element_type=j...  23.7 us
    ppermute x1, waiting for transfers between devices, with_halo(): lax.ppermute(tail, axis, [(i, (i + 1) % count) for i in range(ends)])  13.8 us
  transfers between devices with their start and end apart: 5, of which 4 were waited for; matrix products, arithmetic and copies ran while one was open for 0% of the time, Pallas kernels for 0%

profile of v1, /device:TPU:0, one launch (start us, length us, event | category | flops | bytes accessed | tf_op | source)
XLA Modules:
  0.0 396.4 jit_solution(1716384186507280638)
XLA Ops:
  7.2 2.4 fusion.44
  9.7 3.9 collective-permute-start
  13.6 1.3 collective-permute-start.1
  15.2 0.1 multiply_reduce_fusion
  15.3 0.2 convert_reduce_fusion.1
  15.5 13.8 %collective-permute-done = bf16[2,176,1024]{2,1,0:T(8,128)(2,1)S(1)} collective-permute-done((bf16[2,176,1024]{2,1,0:T(8,128)(2,1)}, bf16[2,176,1024]{2,1,0:T(8,128)(2,1)S(1)}, u32[]{:S(2)}, u32[]{:S(2)}) %collective-permute-start) | collective-permute-done | bytes 720928 | tf_op jit(solution)/shard_map/ppermute | solution.py:28
  29.3 4.1 %collective-permute-done.1 = bf16[2,176,1024]{2,1,0:T(8,128)(2,1)} collective-permute-done((bf16[2,176,1024]{2,1,0:T(8,128)(2,1)S(1)}, bf16[2,176,1024]{2,1,0:T(8,128)(2,1)}, u32[]{:S(2)}, u32[]{:S(2)}) %collective-permute-start.1) | collective-permute-done | bytes 720928 | tf_op jit(solution)/shard_map/ppermute | solution.py:30
  33.4 3.1 pad_maximum_fusion
  36.4 91.2 %while.12 = (s32[]{:T(128)}, bf16[2,176,1024]{2,1,0:T(8,128)(2,1)}, bf16[2,176,4096]{2,1,0:T(8,128)(2,1)}, s32[2]{0:T(128)S(1)}, s32[4096]{0:T(1024)S(1)}, /*ind...) while((s32[]{:T(128)}, bf16[2,176,1024]{2,1,0:T(8,128)(2,1)}, ...), condition=%wide.region_5.6_spmd, body=%wide.region_2.5_spmd.sunk | while | flops 2287300608 | bytes 108356392 | solution.py:93
  36.4 0.7 dynamic_slice.44
  37.8 2.0 broadcast_compare_fusion.2
  39.8 2.1 fusion.61
  41.9 1.6 constant_dynamic-slice_fusion.5
  43.6 1.2 slice.41
  44.8 12.6 %fusion.62 = (f32[2,1024]{1,0:T(2,128)S(1)}, f32[2,1024,3072]{2,1,0:T(8,128)}) fusion(pred[1024,3072]{1,0:T(8,128)(4,1)S(1)} %broadcast_compare_fusion.2, bf16[2,88,1024]{2,1,0:T(8,128)(2,1)S(1)} %bitcast.65, bf16[2,88,3072]{2,1,0:T(8,128)(2,1)} %bitcast.61), kind=kOutput, calls=%fused_computation.3.clone.1 | convolution fusion | flops 1126168576 | bytes 29761536 | tf_op jit(solution)/shard_map/while/body/eval_jaxpr/hdq,hdk->hqk/dot_general | solution.py:78
  57.4 12.0 %fusion.63 = f32[2,1024]{1,0:T(2,128)S(1)} fusion(f32[2,1024,3072]{2,1,0:T(8,128)} %get-tuple-element.157, f32[2,1024]{1,0:T(2,128)S(1)} %get-tuple-element.158, pred[1024,3072]{1,0:T(8,128)(4,1)S(1)} %broadcast_compare_fusion.2), kind=kLoop, calls=%fused_computation.4.clone.1 | loop fusion | flops 25163776 | bytes 28327936 | tf_op jit(solution)/shard_map/while/body/eval_jaxpr/reduce_sum | solution.py:85
  69.4 11.8 %fusion.64 = bf16[2,88,1024]{2,1,0:T(8,128)(2,1)S(1)} fusion(bf16[2,88,3072]{2,1,0:T(8,128)(2,1)S(1)} %bitcast.60, f32[2,1024,3072]{2,1,0:T(8,128)} %get-tuple-element.157, f32[2,1024]{1,0:T(2,128)S(1)} %get-tuple-element.158, pred[1024,3072]{1,0:T(8,128)(4,1)S(1)} %broadcast_compare_fusion.2, f32[2,1024]{1,0:T(2,128)S(1)} %fusion.63), kind=kOutput, calls=%fused_computation.10.clone.1 | convolution fusion | flops 1132822528 | bytes 29769728 | tf_op jit(solution)/shard_map/while/body/eval_jaxpr/hqk,hdk->hdq/dot_general | solution.py:87
  81.3 0.8 bitcast_dynamic-update-slice_fusion.2
  82.0 0.7 dynamic_slice.44
  83.4 2.0 broadcast_compare_fusion.2
  85.4 2.1 fusion.61
  87.5 1.6 constant_dynamic-slice_fusion.5
  89.2 1.2 slice.41
  90.4 12.6 %fusion.62 = (f32[2,1024]{1,0:T(2,128)S(1)}, f32[2,1024,3072]{2,1,0:T(8,128)}) fusion(pred[1024,3072]{1,0:T(8,128)(4,1)S(1)} %broadcast_compare_fusion.2, bf16[2,88,1024]{2,1,0:T(8,128)(2,1)S(1)} %bitcast.65, bf16[2,88,3072]{2,1,0:T(8,128)(2,1)} %bitcast.61), kind=kOutput, calls=%fused_computation.3.clone.1 | convolution fusion | flops 1126168576 | bytes 29761536 | tf_op jit(solution)/shard_map/while/body/eval_jaxpr/hdq,hdk->hqk/dot_general | solution.py:78
  103.0 12.0 %fusion.63 = f32[2,1024]{1,0:T(2,128)S(1)} fusion(f32[2,1024,3072]{2,1,0:T(8,128)} %get-tuple-element.157, f32[2,1024]{1,0:T(2,128)S(1)} %get-tuple-element.158, pred[1024,3072]{1,0:T(8,128)(4,1)S(1)} %broadcast_compare_fusion.2), kind=kLoop, calls=%fused_computation.4.clone.1 | loop fusion | flops 25163776 | bytes 28327936 | tf_op jit(solution)/shard_map/while/body/eval_jaxpr/reduce_sum | solution.py:85
  115.0 11.8 %fusion.64 = bf16[2,88,1024]{2,1,0:T(8,128)(2,1)S(1)} fusion(bf16[2,88,3072]{2,1,0:T(8,128)(2,1)S(1)} %bitcast.60, f32[2,1024,3072]{2,1,0:T(8,128)} %get-tuple-element.157, f32[2,1024]{1,0:T(2,128)S(1)} %get-tuple-element.158, pred[1024,3072]{1,0:T(8,128)(4,1)S(1)} %broadcast_compare_fusion.2, f32[2,1024]{1,0:T(2,128)S(1)} %fusion.63), kind=kOutput, calls=%fused_computation.10.clone.1 | convolution fusion | flops 1132822528 | bytes 29769728 | tf_op jit(solution)/shard_map/while/body/eval_jaxpr/hqk,hdk->hdq/dot_general | solution.py:87
  126.9 0.8 bitcast_dynamic-update-slice_fusion.2
  127.7 1.2 copy.44
  128.8 7.1 %fusion.38 = f32[1408,2048]{1,0:T(8,128)} fusion(bf16[176,2048]{1,0:T(8,128)(2,1)S(1)} %bitcast.66, bf16[1408,1408]{1,0:T(8,128)(2,1)} %param.11, s32[]{:T(128)S(6)} %select_n.41), kind=kOutput, calls=%fused_computation.34 | convolution fusion | flops 1015021568 | bytes 12750852 | tf_op jit(solution)/shard_map/dot_general | solution.py:96
  135.9 0.2 all-gather.3.cloned.1.call-start
  136.2 70.0 %reduce-scatter.2.cloned.1.call-done = f32[176,2048]{1,0:T(8,128)} async-done(((f32[1408,2048]{1,0:T(8,128)}), f32[176,2048]{1,0:T(8,128)}) %reduce-scatter.2.cloned.1.call-update) | async-done | bytes 1441808 | tf_op jit(solution)/shard_map/reduce_scatter | solution.py:99
  206.2 2.4 add_convert_fusion
  208.6 38.4 %all-gather.3.cloned.1.call-done = bf16[1408,2048]{1,0:T(8,128)(2,1)} async-done(((bf16[176,2048]{1,0:T(8,128)(2,1)}), bf16[1408,2048]{1,0:T(8,128)(2,1)}) %all-gather.3.cloned.1.call-update) | async-done | bytes 5767184 | tf_op jit(solution)/shard_map/all_gather | solution.py:101
  247.1 3.7 convert_reduce_fusion
  250.8 0.6 copy-done
  251.4 1.5 fusion.16
  253.0 4.3 %fusion.18 = bf16[1408,2048]{1,0:T(8,128)(2,1)} fusion(bf16[1408,2048]{1,0:T(8,128)(2,1)S(1)} %copy-done, f32[1408]{0:T(1024)S(1)} %copy-done.4, f32[2048]{0:T(1024)S(1)} %add_rsqrt_fusion, f32[2048]{0:T(1024)S(1)} %broadcast_multiply_fusion), kind=kLoop, calls=%fused_computation.23 | loop fusion | flops 14417920 | bytes 11556352 | tf_op jit(solution)/shard_map/convert_element_type | solution.py:105
  257.2 8.4 %copy.37 = bf16[1408,2048]{0,1:T(8,128)(2,1)} copy(bf16[1408,2048]{1,0:T(8,128)(2,1)} %fusion.18) | data formatting | bytes 11534336 | tf_op jit(solution)/shard_map/convert_element_type | solution.py:105
  265.6 10.6 %reshape.124 = bf16[1408,512,4]{0,2,1:T(4,128)(2,1)} reshape(bf16[1408,2048]{0,1:T(8,128)(2,1)} %copy.37) | data formatting | bytes 11534336 | tf_op jit(solution)/shard_map/reshape | solution.py:109
  276.2 4.7 %fusion.33 = bf16[176,512]{1,0:T(8,128)(2,1)S(1)} fusion(bf16[1408,512,4]{0,2,1:T(4,128)(2,1)} %reshape.124, bf16[22,4,8,1408]{3,2,1,0:T(8,128)(2,1)S(1)} %bitcast.72), kind=kOutput, calls=%fused_computation.32 | convolution fusion | flops 1015111680 | bytes 7929856 | tf_op jit(solution)/shard_map/ojf,fgj->og/dot_general | solution.py:111
  281.0 1.9 stack.2
  282.8 6.9 %all-to-all-start = ((bf16[16,176,512]{2,1,0:T(8,128)(2,1)}), bf16[16,176,512]{2,1,0:T(8,128)(2,1)S(1)}, u32[]{:S(2)}, u32[]{:S(2)}) async-start(bf16[16,176,512]{2,1,0:T(8,128)(2,1)} %stack.2), calls=%async_computation.1 | async-start | bytes 5767168 | tf_op jit(solution)/shard_map/all_to_all | solution.py:12
  289.8 56.2 %all-gather = s32[16,1,512]{2,1,0:T(1,128)S(1)} all-gather(s32[1,1,512]{2,1,0:T(1,128)S(1)} %bitcast.70), channel_id=1, replica_groups=mesh['row'=16,'col'=8] {'row'}, dimensions={0}, use_global_device_ids=true | all-gather | bytes 34816 | tf_op jit(solution)/shard_map/all_gather | solution.py:117
  346.0 1.6 copy-done.2
  347.6 2.1 copy.45
  349.8 3.9 copy.41
  353.6 35.2 %scatter_custom_fusion = bf16[176,512]{0,1:T(8,128)(2,1)S(1)} fusion(s32[8192]{0:T(1024)S(1)} %compare_select_fusion, bf16[8192,176]{1,0:T(8,128)(2,1)} %copy.41, bf16[]{:T(256)} %constant.97.clone.1), kind=kCustom, calls=%fused_computation.36 | custom fusion | bytes 180736 | tf_op jit(solution)/shard_map/scatter | solution.py:121
  388.8 0.8 copy.42
  (38 shorter events, 0.5 us)
Async XLA Ops:
  7.2 26.2 %slice-start = ((bf16[3,176,2048]{2,1,0:T(8,128)(2,1)}), bf16[2,176,2048]{2,1,0:T(8,128)(2,1)S(1)}, s32[]{:S(2)}) async-start(bf16[3,176,2048]{2,1,0:T(8,128)(2,1)} %param.9), calls=%async_computation.4 | async-start | bytes 2883584 | tf_op jit(solution)/shard_map/slice | solution.py:58
  7.2 7.8 %copy-start.6 = (s32[64]{0:T(128)S(1)}, s32[64]{0:T(128)}, u32[]{:S(2)}) copy-start(s32[64]{0:T(128)} %param.14) | copy-start | bytes 772
  7.2 199.0 %reduce-scatter.2.cloned.1.call-start = ((), (), s32[]{:S(2)}) async-start(), calls=%async_computation.2 | async-start | bytes 12976128 | tf_op jit(solution)/shard_map/reduce_scatter | solution.py:99
  9.7 19.6 %collective-permute-start = (bf16[2,176,1024]{2,1,0:T(8,128)(2,1)}, bf16[2,176,1024]{2,1,0:T(8,128)(2,1)S(1)}, u32[]{:S(2)}, u32[]{:S(2)}) collective-permute-start(bf16[2,176,1024]{2,1,0:T(8,128)(2,1)} %get-tuple-element.108), channel_id=1, source_target_pairs={{0,8},{8,16},{16,24},{24,32},{32,40},{40,48},{48,56},{56,64},{64,7... | collective-permute-start | bytes 2162696 | tf_op jit(solution)/shard_map/ppermute | solution.py:28
  13.6 19.7 %collective-permute-start.1 = (bf16[2,176,1024]{2,1,0:T(8,128)(2,1)S(1)}, bf16[2,176,1024]{2,1,0:T(8,128)(2,1)}, u32[]{:S(2)}, u32[]{:S(2)}) collective-permute-start(bf16[2,176,1024]{2,1,0:T(8,128)(2,1)S(1)} %get-tuple-element.109), channel_id=1, source_target_pairs={{8,0},{16,8},{24,16},{32,24},{40,32},{48,40},{56,48},{64,56},{72,6... | collective-permute-start | bytes 2162696 | tf_op jit(solution)/shard_map/ppermute | solution.py:30
  57.4 12.0 %copy-start.1 = (bf16[1,176,3072]{2,1,0:T(8,128)(2,1)S(1)}, bf16[1,176,3072]{2,1,0:T(8,128)(2,1)}, u32[]{:S(2)}) copy-start(bf16[1,176,3072]{2,1,0:T(8,128)(2,1)} %get-tuple-element.155) | copy-start | bytes 3244036 | tf_op jit(solution)/shard_map/while
  103.0 12.0 %copy-start.1 = (bf16[1,176,3072]{2,1,0:T(8,128)(2,1)S(1)}, bf16[1,176,3072]{2,1,0:T(8,128)(2,1)}, u32[]{:S(2)}) copy-start(bf16[1,176,3072]{2,1,0:T(8,128)(2,1)} %get-tuple-element.155) | copy-start | bytes 3244036 | tf_op jit(solution)/shard_map/while
  135.9 70.3 %copy-start.3 = (bf16[176,2048]{1,0:T(8,128)(2,1)S(1)}, bf16[176,2048]{1,0:T(8,128)(2,1)}, u32[]{:S(2)}) copy-start(bf16[176,2048]{1,0:T(8,128)(2,1)} %param.10) | copy-start | bytes 2162692
  135.9 111.1 %all-gather.3.cloned.1.call-start = ((), (), s32[]{:S(2)}) async-start(), calls=%async_computation.3 | async-start | bytes 6488064 | tf_op jit(solution)/shard_map/all_gather | solution.py:101
  208.6 44.3 %copy-start.4 = (f32[1408]{0:T(1024)S(1)}, f32[1408]{0:T(1024)}, u32[]{:S(2)}) copy-start(f32[1408]{0:T(1024)} %param.13) | copy-start | bytes 16900
  247.1 4.3 %copy-start = (bf16[1408,2048]{1,0:T(8,128)(2,1)S(1)}, bf16[1408,2048]{1,0:T(8,128)(2,1)}, u32[]{:S(2)}) copy-start(bf16[1408,2048]{1,0:T(8,128)(2,1)} %all-gather.3.cloned.1.call-done) | copy-start | bytes 17301508
  265.6 10.7 %copy-start.7 = (bf16[176,5632]{1,0:T(8,128)(2,1)S(1)}, bf16[176,5632]{1,0:T(8,128)(2,1)}, u32[]{:S(2)}) copy-start(bf16[176,5632]{1,0:T(8,128)(2,1)} %param.12) | copy-start | bytes 5947396
  281.0 8.8 %copy-start.5 = (s32[512]{0:T(512)S(1)}, s32[512]{0:T(512)}, u32[]{:S(2)}) copy-start(s32[512]{0:T(512)} %param.15) | copy-start | bytes 6148
  282.8 63.2 %all-to-all-start = ((bf16[16,176,512]{2,1,0:T(8,128)(2,1)}), bf16[16,176,512]{2,1,0:T(8,128)(2,1)S(1)}, u32[]{:S(2)}, u32[]{:S(2)}) async-start(bf16[16,176,512]{2,1,0:T(8,128)(2,1)} %stack.2), calls=%async_computation.1 | async-start | bytes 5767168 | tf_op jit(solution)/shard_map/all_to_all | solution.py:12
  346.0 1.6 copy-start.2
Sparse Core Ops, SparseCore 0:
  136.1 70.0 reduce-scatter.1
  208.7 38.2 all-gather.2
